TPU v7x, 512 devices: a whole 4x4x16 slice. The times are simulated.
512 devices in a mesh: rows: 128 (over y_hi, z, x), cols: 4 (over y_lo, core).
Axes of the slice: x: 4, y: 4 (y_hi: 2, y_lo: 2; y = y_hi * 2 + y_lo), z: 16, core: 2. Of those that a mesh axis runs over, the one named last changes fastest.
Arguments:
- features: bfloat16 [524288, 256], P('rows', 'cols'), may hold values from -6 to 6
- weight: bfloat16 [256, 256], P(None, 'cols'), may hold values from -0.375 to 0.375
- tile_values: bfloat16 [11264, 128, 128], P('rows'), as said below
- tile_rows: int32 [11264], P('rows'), may hold values from 0 to 31
- tile_cols: int32 [11264], P('rows'), may hold values from 0 to 159, as said below
- tile_count: int32 [128], P('rows'), may hold values from 44 to 88, as said below
- cotangent: bfloat16 [524288, 256], P('rows', 'cols'), may hold values from -6 to 6
Outputs:
- output: bfloat16 [524288, 256], P('rows', 'cols')
- feature_grad: bfloat16 [524288, 256], P('rows', 'cols')
- weight_grad: float32 [256, 256], P(None, 'cols')
Inputs may be any that keep to these rules, and one draw needn't show every extreme that they name: `tile_count`: live tile slots of a partition, at least 44; some partition has all 88 slots live in every draw. `tile_cols`: slot s of a partition (counted from the partition's first slot) draws its source from the partition (s mod 5) - 2 steps away around the loop, so c div (32) = s mod 5. `tile_values`: edge weights are zero or positive.
All inputs are finite; a program needn't handle non-finite values.
Results may differ from a plain program's by a relative error of at most 0.02.
Values may be sent and summed in bfloat16 or wider, within the bound.
No kernel may reach another device: no remote copies, remote signals or barrier semaphores. Data moves between devices by JAX's collectives and lax.ppermute only.
A program may use at most 64 MiB of HBM per device.

v0:
```python
import jax
import jax.numpy as jnp
from jax import lax
from jax.sharding import PartitionSpec as P


def passed_along(value, axis, steps):
    count = lax.axis_size(axis)
    pairs = [(source, (source + steps) % count) for source in range(count)]
    return lax.ppermute(value, axis, pairs)


def silu_grad(value):
    sigmoid_val = jax.nn.sigmoid(value)
    return sigmoid_val * (1.0 + value * (1.0 - sigmoid_val))


def local(features, weight, tile_values, tile_rows, tile_cols, tile_count, cotangent):
    node_count, feat_cols = features.shape
    slot_count, tile_size = (tile_values.shape[0], tile_values.shape[1])
    block_count = node_count // tile_size
    block_ids = jnp.arange(block_count, dtype=jnp.int32)
    live_slots = (jnp.arange(slot_count, dtype=jnp.int32) < tile_count[0]).astype(jnp.float32)
    going_down = features
    going_up = features
    lower_blocks = []
    upper_blocks = []
    for section in range(2):
        going_down = passed_along(going_down, "rows", 1)
        lower_blocks.append(going_down)
        going_up = passed_along(going_up, "rows", -1)
        upper_blocks.append(going_up)
    band_rows = jnp.concatenate(
        [lower_blocks[1], lower_blocks[0], features, upper_blocks[0], upper_blocks[1]], 0
    )
    band_rows = band_rows.reshape(5 * block_count, tile_size, feat_cols)
    source = band_rows[tile_cols]
    products = (
        jnp.einsum("tij,tjf->tif", tile_values, source, preferred_element_type=jnp.float32)
        * live_slots[:, None, None]
    )
    row_select = (tile_rows[None, :] == block_ids[:, None]).astype(jnp.float32)
    hidden_part = (
        jnp.einsum("bt,tif->bif", row_select, products)
        .reshape(node_count, feat_cols)
        .astype(jnp.bfloat16)
    )
    hidden = lax.all_gather(hidden_part, "cols", axis=1, tiled=True)
    preact = jnp.dot(hidden, weight, preferred_element_type=jnp.float32)
    output = jax.nn.silu(preact).astype(jnp.bfloat16)
    grad_pre = (cotangent.astype(jnp.float32) * silu_grad(preact)).astype(jnp.bfloat16)
    total_nodes = node_count * lax.axis_size("rows")
    weight_term = lax.dot_general(
        hidden, grad_pre, (((0,), (0,)), ((), ())), preferred_element_type=jnp.float32
    )
    weight_grad = lax.psum(weight_term, "rows") * (1.0 / total_nodes**0.5)
    partial_terms = lax.dot_general(
        grad_pre, weight, (((1,), (1,)), ((), ())), preferred_element_type=jnp.float32
    )
    hidden_grad = lax.psum_scatter(
        partial_terms.astype(jnp.bfloat16), "cols", scatter_dimension=1, tiled=True
    )
    grad_blocks = hidden_grad.reshape(block_count, tile_size, feat_cols)
    grad_source = grad_blocks[tile_rows]
    contrib = (
        jnp.einsum("tji,tjf->tif", tile_values, grad_source, preferred_element_type=jnp.float32)
        * live_slots[:, None, None]
    )
    band_select = (
        tile_cols[None, :] == jnp.arange(5 * block_count, dtype=jnp.int32)[:, None]
    ).astype(jnp.float32)
    outgoing = jnp.einsum("ct,tif->cif", band_select, contrib).reshape(5, node_count, feat_cols)
    moving_up = outgoing[4]
    moving_down = outgoing[0]
    for section in range(2):
        moving_up = passed_along(moving_up.astype(jnp.bfloat16), "rows", 1).astype(moving_up.dtype)
        moving_down = passed_along(moving_down.astype(jnp.bfloat16), "rows", -1).astype(
            moving_down.dtype
        )
        if section == 0:
            moving_up = moving_up + outgoing[3]
            moving_down = moving_down + outgoing[1]
    gathered = outgoing[2] + moving_up + moving_down
    feature_grad = gathered.astype(jnp.bfloat16)
    return (output, feature_grad, weight_grad)


def solution(mesh):
    in_specs = (
        P("rows", "cols"),
        P(None, "cols"),
        P("rows", None, None),
        P("rows"),
        P("rows"),
        P("rows"),
        P("rows", "cols"),
    )
    out_specs = (P("rows", "cols"), P("rows", "cols"), P(None, "cols"))
    return jax.shard_map(local, mesh=mesh, in_specs=in_specs, out_specs=out_specs, check_vma=False)
```

profile of v0, /device:TPU:8, one launch (start us, length us, event | category | flops | bytes accessed | tf_op | source)
XLA Modules:
  0.0 1374.6 jit_solution(18113469015568557949)
XLA Ops:
  7.2 3.7 collective-permute-start
  10.9 13.9 %collective-permute-start.2 = (bf16[4096,64]{0,1:T(8,128)(2,1)}, bf16[4096,64]{0,1:T(8,128)(2,1)S(1)}, u32[]{:S(2)}, u32[]{:S(2)}) collective-permute-start(bf16[4096,64]{0,1:T(8,128)(2,1)} %param.7), channel_id=1, source_target_pairs={{0,508},{4,0},{8,4},{12,8},{16,12},{20,16},{24,20},{28,24},{32,28}... | collective-permute-start | bytes 1572872 | tf_op jit(solution)/shard_map/ppermute | solution.py:10
  24.8 10.2 collective-permute-done
  34.9 1.9 collective-permute-start.1
  38.2 9.6 collective-permute-start.3
  47.8 7.8 collective-permute-done.1
  58.2 2.3 copy_bitcast_fusion
  60.5 3.7 gather_fusion
  64.1 3.5 multiply_bitcast_fusion.1
  69.7 29.8 %all-gather.2.cloned.1.call-done = bf16[4096,256]{0,1:T(8,128)(2,1)} async-done(((bf16[4096,64]{0,1:T(8,128)(2,1)}), bf16[4096,256]{0,1:T(8,128)(2,1)}) %all-gather.2.cloned.1.call-update) | async-done | bytes 2097168 | tf_op jit(solution)/shard_map/all_gather | solution.py:48
  99.5 3.2 multiply_convert_fusion
  103.5 2.0 convolution_convert_fusion
  105.7 37.0 %reduce-scatter.2.cloned.1.call-done = bf16[4096,64]{0,1:T(8,128)(2,1)} async-done(((bf16[4096,256]{0,1:T(8,128)(2,1)}), bf16[4096,64]{0,1:T(8,128)(2,1)}) %reduce-scatter.2.cloned.1.call-update) | async-done | bytes 524304 | tf_op jit(solution)/shard_map/reduce_scatter | solution.py:60
  143.8 1.9 gather_fusion.1
  145.7 2.3 multiply_bitcast_fusion
  148.0 1.6 fusion.19
  149.9 10.7 collective-permute-start.6
  160.8 1.9 collective-permute-start.4
  164.0 8.0 collective-permute-done.6
  173.4 10.1 collective-permute-start.7
  184.9 1.9 collective-permute-start.5
  188.2 1175.6 %all-reduce.2.cloned.1.call-done = f32[256,64]{0,1:T(8,128)} async-done(((f32[256,64]{0,1:T(8,128)}), f32[256,64]{0,1:T(8,128)}) %all-reduce.2.cloned.1.call-update) | async-done | bytes 65552 | tf_op jit(solution)/shard_map/psum | solution.py:56
  1363.8 1.5 broadcast_multiply_fusion
  1365.3 2.8 fusion.10
  (45 shorter events, 13.4 us)
Async XLA Ops:
  7.2 57.0 %copy-start = (bf16[88,128,128]{2,1,0:T(8,128)(2,1)S(1)}, bf16[88,128,128]{2,1,0:T(8,128)(2,1)}, u32[]{:S(2)}) copy-start(bf16[88,128,128]{2,1,0:T(8,128)(2,1)} %param.9) | copy-start | bytes 8650756
  7.2 92.3 %all-gather.2.cloned.1.call-start = ((), (), s32[]{:S(2)}) async-start(), calls=%async_computation.1 | async-start | bytes 2621440 | tf_op jit(solution)/shard_map/all_gather | solution.py:48
  7.2 27.7 %collective-permute-start = (bf16[4096,64]{0,1:T(8,128)(2,1)}, bf16[4096,64]{0,1:T(8,128)(2,1)S(1)}, u32[]{:S(2)}, u32[]{:S(2)}) collective-permute-start(bf16[4096,64]{0,1:T(8,128)(2,1)} %param.7), channel_id=1, source_target_pairs={{0,4},{4,8},{8,12},{12,16},{16,20},{20,24},{24,28},{28,32},{32,36}... | collective-permute-start | bytes 1572872 | tf_op jit(solution)/shard_map/ppermute | solution.py:10
  10.9 27.3 %collective-permute-start.2 = (bf16[4096,64]{0,1:T(8,128)(2,1)}, bf16[4096,64]{0,1:T(8,128)(2,1)S(1)}, u32[]{:S(2)}, u32[]{:S(2)}) collective-permute-start(bf16[4096,64]{0,1:T(8,128)(2,1)} %param.7), channel_id=1, source_target_pairs={{0,508},{4,0},{8,4},{12,8},{16,12},{20,16},{24,20},{28,24},{32,28}... | collective-permute-start | bytes 1572872 | tf_op jit(solution)/shard_map/ppermute | solution.py:10
  34.9 20.7 %collective-permute-start.1 = (bf16[4096,64]{0,1:T(8,128)(2,1)S(1)}, bf16[4096,64]{0,1:T(8,128)(2,1)S(1)}, u32[]{:S(2)}, u32[]{:S(2)}) collective-permute-start(bf16[4096,64]{0,1:T(8,128)(2,1)S(1)} %collective-permute-done), channel_id=1, source_target_pairs={{0,4},{4,8},{8,12},{12,16},{16,20},{20,24},{24,28},{28,32},{32,36}... | collective-permute-start | bytes 1572872 | tf_op jit(solution)/shard_map/ppermute | solution.py:10
  38.2 20.0 %collective-permute-start.3 = (bf16[4096,64]{0,1:T(8,128)(2,1)S(1)}, bf16[4096,64]{0,1:T(8,128)(2,1)S(1)}, u32[]{:S(2)}, u32[]{:S(2)}) collective-permute-start(bf16[4096,64]{0,1:T(8,128)(2,1)S(1)} %collective-permute-done.2), channel_id=1, source_target_pairs={{0,508},{4,0},{8,4},{12,8},{16,12},{20,16},{24,20},{28,24},{32,28}... | collective-permute-start | bytes 1572872 | tf_op jit(solution)/shard_map/ppermute | solution.py:10
  64.1 3.5 copy-start.5
  67.6 31.9 %copy-start.4 = (bf16[256,64]{0,1:T(8,128)(2,1)S(1)}, bf16[256,64]{0,1:T(8,128)(2,1)}, u32[]{:S(2)}) copy-start(bf16[256,64]{0,1:T(8,128)(2,1)} %param.8) | copy-start | bytes 98308
  69.7 72.9 %reduce-scatter.2.cloned.1.call-start = ((), (), s32[]{:S(2)}) async-start(), calls=%async_computation.2 | async-start | bytes 2621440 | tf_op jit(solution)/shard_map/reduce_scatter | solution.py:60
  102.7 0.8 copy-start.2
  105.6 1258.2 %all-reduce.2.cloned.1.call-start = ((), (), s32[]{:S(2)}) async-start(), calls=%async_computation.3 | async-start | bytes 131072 | tf_op jit(solution)/shard_map/psum | solution.py:56
  145.7 2.3 copy-start.6
  149.9 22.1 %collective-permute-start.6 = (bf16[4096,64]{0,1:T(8,128)(2,1)S(1)}, bf16[4096,64]{0,1:T(8,128)(2,1)S(1)}, u32[]{:S(2)}, u32[]{:S(2)}) collective-permute-start(bf16[4096,64]{0,1:T(8,128)(2,1)S(1)} %bitcast.83), channel_id=1, source_target_pairs={{0,508},{4,0},{8,4},{12,8},{16,12},{20,16},{24,20},{28,24},{32,28}... | collective-permute-start | bytes 1572872 | tf_op jit(solution)/shard_map/ppermute | solution.py:10
  160.8 22.7 %collective-permute-start.4 = (bf16[4096,64]{0,1:T(8,128)(2,1)S(1)}, bf16[4096,64]{0,1:T(8,128)(2,1)S(1)}, u32[]{:S(2)}, u32[]{:S(2)}) collective-permute-start(bf16[4096,64]{0,1:T(8,128)(2,1)S(1)} %bitcast.82), channel_id=1, source_target_pairs={{0,4},{4,8},{8,12},{12,16},{16,20},{20,24},{24,28},{28,32},{32,36}... | collective-permute-start | bytes 1572872 | tf_op jit(solution)/shard_map/ppermute | solution.py:10
  164.0 22.8 %copy-start.1 = (bf16[4096,256]{0,1:T(8,128)(2,1)S(1)}, bf16[4096,256]{0,1:T(8,128)(2,1)}, u32[]{:S(2)}) copy-start(bf16[4096,256]{0,1:T(8,128)(2,1)} %all-gather.2.cloned.1.call-done) | copy-start | bytes 6291460
  164.0 22.8 %copy-start.3 = (bf16[4096,64]{0,1:T(8,128)(2,1)S(1)}, bf16[4096,64]{0,1:T(8,128)(2,1)}, u32[]{:S(2)}) copy-start(bf16[4096,64]{0,1:T(8,128)(2,1)} %copy-done.2) | copy-start | bytes 1572868
  173.4 1191.9 %collective-permute-start.7 = (bf16[4096,64]{0,1:T(8,128)(2,1)}, bf16[4096,64]{0,1:T(8,128)(2,1)S(1)}, u32[]{:S(2)}, u32[]{:S(2)}) collective-permute-start(bf16[4096,64]{0,1:T(8,128)(2,1)} %fusion.7), channel_id=1, source_target_pairs={{0,508},{4,0},{8,4},{12,8},{16,12},{20,16},{24,20},{28,24},{32,28}... | collective-permute-start | bytes 1572872 | tf_op jit(solution)/shard_map/ppermute | solution.py:10
  184.9 1180.4 %collective-permute-start.5 = (bf16[4096,64]{0,1:T(8,128)(2,1)}, bf16[4096,64]{0,1:T(8,128)(2,1)}, u32[]{:S(2)}, u32[]{:S(2)}) collective-permute-start(bf16[4096,64]{0,1:T(8,128)(2,1)} %fusion.8), channel_id=1, source_target_pairs={{0,4},{4,8},{8,12},{12,16},{16,20},{20,24},{24,28},{28,32},{32,36}... | collective-permute-start | bytes 1572872 | tf_op jit(solution)/shard_map/ppermute | solution.py:10
Sparse Core Ops, SparseCore 0:
  69.8 29.6 all-gather.1
  105.7 36.8 reduce-scatter.1
  188.4 1175.4 all-reduce.1
where the time goes:
time: 1380 us; the launch traced here: 1370 us
  waiting for transfers between devices  1270 us (92%)
  starting transfers between devices  53.8 us (4%)
  matrix products  15 us (1%)
  between operations  14.6 us (1%)
  local copies, waits for them, and re-layouts  13.9 us (1%)
    psum x1, waiting for transfers between devices, local(): weight_grad = lax.psum(weight_term, 'rows') * (1.0 / total_nodes ** 0.5)  1180 us
    ppermute x8, starting transfers between devices, passed_along(): return lax.ppermute(value, axis, pairs)  53.7 us
    reduce_scatter x1, waiting for transfers between devices, local(): lax.psum_scatter(partial_terms.astype(jnp.bfloat16), 'cols', scatter_dime...  37 us
    all_gather x1, waiting for transfers between devices, local(): hidden = lax.all_gather(hidden_part, 'cols', axis=1, tiled=True)  29.8 us
  transfers between devices with their start and end apart: 11, of which 7 were waited for; matrix products, arithmetic and copies ran while one was open for 1% of the time, Pallas kernels for 0%

commit v1 on v0

--- a/solution.py
+++ b/solution.py
@@ -53,7 +53,7 @@
     weight_term = lax.dot_general(
         hidden, grad_pre, (((0,), (0,)), ((), ())), preferred_element_type=jnp.float32
     )
-    weight_grad = lax.psum(weight_term, "rows") * (1.0 / total_nodes**0.5)
+    weight_grad = jnp.sum(lax.all_gather(weight_term, "rows"), axis=0) * (1.0 / total_nodes**0.5)
     partial_terms = lax.dot_general(
         grad_pre, weight, (((1,), (1,)), ((), ())), preferred_element_type=jnp.float32
     )

time: 1380 us -> 404 us (0.29)
  the two profiles are of different devices: /device:TPU:8 before, /device:TPU:2 now
where the time goes in v1:
time: 404 us; the launch traced here: 403 us
  waiting for transfers between devices  305 us (75%)
  starting transfers between devices  43.5 us (11%)
  local copies, waits for them, and re-layouts  18 us (4%)
  matrix products  16.6 us (4%)
  between operations  14.6 us (4%)
  other arithmetic  5.66 us (1%)
    all_gather x1, waiting for transfers between devices, local(): lax.all_gather(weight_term, 'rows')  189 us
    ppermute x8, waiting for transfers between devices, passed_along(): return lax.ppermute(value, axis, pairs)  44.2 us
    ppermute x8, starting transfers between devices, passed_along(): return lax.ppermute(value, axis, pairs)  43.4 us
    all_gather x1, waiting for transfers between devices, local(): hidden = lax.all_gather(hidden_part, 'cols', axis=1, tiled=True)  37.4 us
    reduce_scatter x1, waiting for transfers between devices, local(): lax.psum_scatter(partial_terms.astype(jnp.bfloat16), 'cols', scatter_dime...  34.1 us
    unnamed x16, local copies, waits for them, and re-layouts  8.51 us
  transfers between devices with their start and end apart: 11, of which 10 were waited for; matrix products, arithmetic and copies ran while one was open for 4% of the time, Pallas kernels for 0%

profile of v1, /device:TPU:2, one launch (start us, length us, event | category | flops | bytes accessed | tf_op | source)
XLA Modules:
  0.0 402.9 jit_solution(8314580286726726792)
XLA Ops:
  7.2 3.7 collective-permute-start
  10.9 6.3 %collective-permute-start.2 = (bf16[4096,64]{0,1:T(8,128)(2,1)}, bf16[4096,64]{0,1:T(8,128)(2,1)S(1)}, u32[]{:S(2)}, u32[]{:S(2)}) collective-permute-start(bf16[4096,64]{0,1:T(8,128)(2,1)} %param.7), channel_id=1, source_target_pairs={{0,508},{4,0},{8,4},{12,8},{16,12},{20,16},{24,20},{28,24},{32,28}... | collective-permute-start | bytes 1572872 | tf_op jit(solution)/shard_map/ppermute | solution.py:10
  17.2 6.0 %collective-permute-done = bf16[4096,64]{0,1:T(8,128)(2,1)S(1)} collective-permute-done((bf16[4096,64]{0,1:T(8,128)(2,1)}, bf16[4096,64]{0,1:T(8,128)(2,1)S(1)}, u32[]{:S(2)}, u32[]{:S(2)}) %collective-permute-start) | collective-permute-done | bytes 524320 | tf_op jit(solution)/shard_map/ppermute | solution.py:10
  23.3 3.4 collective-permute-start.1
  28.0 13.6 %collective-permute-start.3 = (bf16[4096,64]{0,1:T(8,128)(2,1)S(1)}, bf16[4096,64]{0,1:T(8,128)(2,1)S(1)}, u32[]{:S(2)}, u32[]{:S(2)}) collective-permute-start(bf16[4096,64]{0,1:T(8,128)(2,1)S(1)} %collective-permute-done.2), channel_id=1, source_target_pairs={{0,508},{4,0},{8,4},{12,8},{16,12},{20,16},{24,20},{28,24},{32,28}... | collective-permute-start | bytes 1572872 | tf_op jit(solution)/shard_map/ppermute | solution.py:10
  41.5 8.1 %collective-permute-done.1 = bf16[4096,64]{0,1:T(8,128)(2,1)S(1)} collective-permute-done((bf16[4096,64]{0,1:T(8,128)(2,1)S(1)}, bf16[4096,64]{0,1:T(8,128)(2,1)S(1)}, u32[]{:S(2)}, u32[]{:S(2)}) %collective-permute-start.1) | collective-permute-done | bytes 524320 | tf_op jit(solution)/shard_map/ppermute | solution.py:10
  52.2 2.2 copy_bitcast_fusion
  54.4 3.7 gather_fusion
  58.1 3.5 multiply_bitcast_fusion.1
  63.7 37.4 %all-gather.4.cloned.1.call-done = bf16[4096,256]{0,1:T(8,128)(2,1)} async-done(((bf16[4096,64]{0,1:T(8,128)(2,1)}), bf16[4096,256]{0,1:T(8,128)(2,1)}) %all-gather.4.cloned.1.call-update) | async-done | bytes 2097168 | tf_op jit(solution)/shard_map/all_gather | solution.py:48
  101.1 3.2 multiply_convert_fusion
  104.3 2.1 convolution_convert_fusion
  106.5 3.0 fusion.20
  109.6 34.1 %reduce-scatter.2.cloned.1.call-done = bf16[4096,64]{0,1:T(8,128)(2,1)} async-done(((bf16[4096,256]{0,1:T(8,128)(2,1)}), bf16[4096,64]{0,1:T(8,128)(2,1)}) %reduce-scatter.2.cloned.1.call-update) | async-done | bytes 524304 | tf_op jit(solution)/shard_map/reduce_scatter | solution.py:60
  146.8 2.3 multiply_bitcast_fusion
  150.9 2.5 collective-permute-start.6
  153.6 3.4 collective-permute-start.4
  157.3 9.4 %collective-permute-done.6 = bf16[4096,64]{0,1:T(8,128)(2,1)S(1)} collective-permute-done((bf16[4096,64]{0,1:T(8,128)(2,1)S(1)}, bf16[4096,64]{0,1:T(8,128)(2,1)S(1)}, u32[]{:S(2)}, u32[]{:S(2)}) %collective-permute-start.6) | collective-permute-done | bytes 524320 | tf_op jit(solution)/shard_map/ppermute | solution.py:10
  167.4 8.5 %collective-permute-start.7 = (bf16[4096,64]{0,1:T(8,128)(2,1)S(1)}, bf16[4096,64]{0,1:T(8,128)(2,1)S(1)}, u32[]{:S(2)}, u32[]{:S(2)}) collective-permute-start(bf16[4096,64]{0,1:T(8,128)(2,1)S(1)} %fusion.7), channel_id=1, source_target_pairs={{0,508},{4,0},{8,4},{12,8},{16,12},{20,16},{24,20},{28,24},{32,28}... | collective-permute-start | bytes 1572872 | tf_op jit(solution)/shard_map/ppermute | solution.py:10
  176.7 2.1 collective-permute-start.5
  178.8 7.8 %collective-permute-done.7 = bf16[4096,64]{0,1:T(8,128)(2,1)S(1)} collective-permute-done((bf16[4096,64]{0,1:T(8,128)(2,1)S(1)}, bf16[4096,64]{0,1:T(8,128)(2,1)S(1)}, u32[]{:S(2)}, u32[]{:S(2)}) %collective-permute-start.7) | collective-permute-done | bytes 524320 | tf_op jit(solution)/shard_map/ppermute | solution.py:10
  186.6 11.4 %collective-permute-done.5 = bf16[4096,64]{0,1:T(8,128)(2,1)S(1)} collective-permute-done((bf16[4096,64]{0,1:T(8,128)(2,1)S(1)}, bf16[4096,64]{0,1:T(8,128)(2,1)S(1)}, u32[]{:S(2)}, u32[]{:S(2)}) %collective-permute-start.5) | collective-permute-done | bytes 524320 | tf_op jit(solution)/shard_map/ppermute | solution.py:10
  199.5 188.8 %all-gather.6.cloned.1.call-done = f32[32768,64]{0,1:T(8,128)} async-done(((f32[256,64]{0,1:T(8,128)}), f32[32768,64]{0,1:T(8,128)}) %all-gather.6.cloned.1.call-update) | async-done | bytes 8388624 | tf_op jit(solution)/shard_map/all_gather | solution.py:56
  388.3 5.9 %copy.23 = f32[8,8,128,256]{3,2,1,0:T(8,128)S(1)} copy(f32[8,8,128,256]{3,1,2,0:T(8,128)} %bitcast.80) | data formatting | bytes 16777216
  (41 shorter events, 16.0 us)
Async XLA Ops:
  7.2 50.9 %copy-start = (bf16[88,128,128]{2,1,0:T(8,128)(2,1)S(1)}, bf16[88,128,128]{2,1,0:T(8,128)(2,1)}, u32[]{:S(2)}) copy-start(bf16[88,128,128]{2,1,0:T(8,128)(2,1)} %param.9) | copy-start | bytes 8650756
  7.2 93.9 %all-gather.4.cloned.1.call-start = ((), (), s32[]{:S(2)}) async-start(), calls=%async_computation.1 | async-start | bytes 2621440 | tf_op jit(solution)/shard_map/all_gather | solution.py:48
  7.2 16.0 %collective-permute-start = (bf16[4096,64]{0,1:T(8,128)(2,1)}, bf16[4096,64]{0,1:T(8,128)(2,1)S(1)}, u32[]{:S(2)}, u32[]{:S(2)}) collective-permute-start(bf16[4096,64]{0,1:T(8,128)(2,1)} %param.7), channel_id=1, source_target_pairs={{0,4},{4,8},{8,12},{12,16},{16,20},{20,24},{24,28},{28,32},{32,36}... | collective-permute-start | bytes 1572872 | tf_op jit(solution)/shard_map/ppermute | solution.py:10
  10.9 17.1 %collective-permute-start.2 = (bf16[4096,64]{0,1:T(8,128)(2,1)}, bf16[4096,64]{0,1:T(8,128)(2,1)S(1)}, u32[]{:S(2)}, u32[]{:S(2)}) collective-permute-start(bf16[4096,64]{0,1:T(8,128)(2,1)} %param.7), channel_id=1, source_target_pairs={{0,508},{4,0},{8,4},{12,8},{16,12},{20,16},{24,20},{28,24},{32,28}... | collective-permute-start | bytes 1572872 | tf_op jit(solution)/shard_map/ppermute | solution.py:10
  23.3 26.4 %collective-permute-start.1 = (bf16[4096,64]{0,1:T(8,128)(2,1)S(1)}, bf16[4096,64]{0,1:T(8,128)(2,1)S(1)}, u32[]{:S(2)}, u32[]{:S(2)}) collective-permute-start(bf16[4096,64]{0,1:T(8,128)(2,1)S(1)} %collective-permute-done), channel_id=1, source_target_pairs={{0,4},{4,8},{8,12},{12,16},{16,20},{20,24},{24,28},{28,32},{32,36}... | collective-permute-start | bytes 1572872 | tf_op jit(solution)/shard_map/ppermute | solution.py:10
  28.0 24.2 %collective-permute-start.3 = (bf16[4096,64]{0,1:T(8,128)(2,1)S(1)}, bf16[4096,64]{0,1:T(8,128)(2,1)S(1)}, u32[]{:S(2)}, u32[]{:S(2)}) collective-permute-start(bf16[4096,64]{0,1:T(8,128)(2,1)S(1)} %collective-permute-done.2), channel_id=1, source_target_pairs={{0,508},{4,0},{8,4},{12,8},{16,12},{20,16},{24,20},{28,24},{32,28}... | collective-permute-start | bytes 1572872 | tf_op jit(solution)/shard_map/ppermute | solution.py:10
  58.1 3.5 copy-start.2
  61.6 39.5 %copy-start.1 = (bf16[256,64]{0,1:T(8,128)(2,1)S(1)}, bf16[256,64]{0,1:T(8,128)(2,1)}, u32[]{:S(2)}) copy-start(bf16[256,64]{0,1:T(8,128)(2,1)} %param.8) | copy-start | bytes 98308
  63.7 80.0 %reduce-scatter.2.cloned.1.call-start = ((), (), s32[]{:S(2)}) async-start(), calls=%async_computation.2 | async-start | bytes 2621440 | tf_op jit(solution)/shard_map/reduce_scatter | solution.py:60
  106.5 281.9 %all-gather.6.cloned.1.call-start = ((), (), s32[]{:S(2)}) async-start(), calls=%async_computation.3 | async-start | bytes 8454144 | tf_op jit(solution)/shard_map/all_gather | solution.py:56
  146.8 2.3 copy-start.3
  150.9 15.8 %collective-permute-start.6 = (bf16[4096,64]{0,1:T(8,128)(2,1)S(1)}, bf16[4096,64]{0,1:T(8,128)(2,1)S(1)}, u32[]{:S(2)}, u32[]{:S(2)}) collective-permute-start(bf16[4096,64]{0,1:T(8,128)(2,1)S(1)} %bitcast.89), channel_id=1, source_target_pairs={{0,508},{4,0},{8,4},{12,8},{16,12},{20,16},{24,20},{28,24},{32,28}... | collective-permute-start | bytes 1572872 | tf_op jit(solution)/shard_map/ppermute | solution.py:10
  153.6 22.4 %collective-permute-start.4 = (bf16[4096,64]{0,1:T(8,128)(2,1)S(1)}, bf16[4096,64]{0,1:T(8,128)(2,1)S(1)}, u32[]{:S(2)}, u32[]{:S(2)}) collective-permute-start(bf16[4096,64]{0,1:T(8,128)(2,1)S(1)} %bitcast.88), channel_id=1, source_target_pairs={{0,4},{4,8},{8,12},{12,16},{16,20},{20,24},{24,28},{28,32},{32,36}... | collective-permute-start | bytes 1572872 | tf_op jit(solution)/shard_map/ppermute | solution.py:10
  167.4 19.2 %collective-permute-start.7 = (bf16[4096,64]{0,1:T(8,128)(2,1)S(1)}, bf16[4096,64]{0,1:T(8,128)(2,1)S(1)}, u32[]{:S(2)}, u32[]{:S(2)}) collective-permute-start(bf16[4096,64]{0,1:T(8,128)(2,1)S(1)} %fusion.7), channel_id=1, source_target_pairs={{0,508},{4,0},{8,4},{12,8},{16,12},{20,16},{24,20},{28,24},{32,28}... | collective-permute-start | bytes 1572872 | tf_op jit(solution)/shard_map/ppermute | solution.py:10
  176.7 21.4 %collective-permute-start.5 = (bf16[4096,64]{0,1:T(8,128)(2,1)S(1)}, bf16[4096,64]{0,1:T(8,128)(2,1)S(1)}, u32[]{:S(2)}, u32[]{:S(2)}) collective-permute-start(bf16[4096,64]{0,1:T(8,128)(2,1)S(1)} %fusion.8), channel_id=1, source_target_pairs={{0,4},{4,8},{8,12},{12,16},{16,20},{20,24},{24,28},{28,32},{32,36}... | collective-permute-start | bytes 1572872 | tf_op jit(solution)/shard_map/ppermute | solution.py:10
Sparse Core Ops, SparseCore 0:
  63.8 37.2 all-gather.3
  106.6 37.0 reduce-scatter.1
  149.3 238.9 all-gather.5
